TPU v7x, 256 devices: a whole 4x4x8 slice. The times are simulated.
256 devices in a mesh: dp: 32 (over z, x_hi, core), tensor: 8 (over y, x_lo).
Axes of the slice: x: 4 (x_hi: 2, x_lo: 2; x = x_hi * 2 + x_lo), y: 4, z: 8, core: 2. Of those that a mesh axis runs over, the one named last changes fastest.
Arguments:
- context: bfloat16 [12288, 8192], P('dp', 'tensor'), may hold values from -6 to 6
- output_weight: bfloat16 [8192, 8192], P('tensor', 'dp'), may hold values from -0.0625 to 0.0625
- adapter_down_weight: bfloat16 [8192, 16], P('tensor'), may hold values from -0.0625 to 0.0625
- adapter_up_weight: bfloat16 [16, 8192], replicated, may hold values from -0.29882812 to 0.29882812
- residual: bfloat16 [12288, 8192], P('dp', 'tensor'), may hold values from -60 to 60
- frozen_residual_delta: bfloat16 [12288, 8192], P('dp', 'tensor'), may hold values from -6 to 6
- harmful_count: int32 [32], replicated, may hold values from 48 to 192
- retain_count: int32 [32], replicated, may hold values from 48 to 192
Outputs:
- adapted: bfloat16 [12288, 8192], P('dp', 'tensor')
- grad_a: float32 [8192, 16], P('tensor')
- grad_b: float32 [16, 8192], replicated
All inputs are finite; a program needn't handle non-finite values.
Results may differ from a plain program's by a relative error of at most 0.005.
Values may be sent and summed in bfloat16 or wider, within the bound.
A program may use at most 128 MiB of HBM per device.

v0:
```python
import jax
import jax.numpy as jnp
from jax import lax
from jax.sharding import PartitionSpec as P

ADAPTER_SCALE = 2.0
NORM_EPS = 1e-06
REROUTE_WEIGHT = 65536.0
RETAIN_WEIGHT = 1024.0


def row_gradient(
    hidden_states,
    target,
    sq_state,
    sq_target,
    cross_term,
    gap_sq,
    harmful,
    retained,
    harm_total,
    keep_total,
):
    norm_h = jnp.sqrt(sq_state + NORM_EPS)
    norm_g = jnp.sqrt(sq_target + NORM_EPS)
    cosine = cross_term / (norm_h * norm_g)
    distance = jnp.sqrt(gap_sq + NORM_EPS)
    weight_harm = REROUTE_WEIGHT / harm_total * harmful
    weight_keep = RETAIN_WEIGHT / keep_total * retained
    first = (weight_harm / (norm_h * norm_g))[:, None] * target
    second = (weight_harm * cosine / (norm_h * norm_h))[:, None] * hidden_states
    third = (weight_keep / distance)[:, None] * (hidden_states - target)
    return first - second + third


def token_masks(positions, harm_here, keep_here):
    harmful = (positions < harm_here).astype(jnp.float32)
    retained = ((positions >= harm_here) & (positions < harm_here + keep_here)).astype(jnp.float32)
    return (harmful, retained)


def head_terms(context, output_weight):
    return jnp.dot(
        context,
        lax.all_gather(output_weight, "dp", axis=1, tiled=True),
        preferred_element_type=jnp.float32,
    )


def local(
    context,
    output_weight,
    adapter_down_weight,
    adapter_up_weight,
    residual,
    frozen_residual_delta,
    harmful_count,
    retain_count,
):
    seq_len = context.shape[0]
    tensor_rank = lax.axis_index("tensor")
    data_rank = lax.axis_index("dp")
    harm_total = jnp.sum(harmful_count).astype(jnp.float32)
    keep_total = jnp.sum(retain_count).astype(jnp.float32)
    harm_here = harmful_count[data_rank]
    keep_here = retain_count[data_rank]
    up_weight_single = adapter_up_weight.astype(jnp.float32)
    reduced_state = lax.psum(
        jnp.dot(context, adapter_down_weight, preferred_element_type=jnp.float32), "tensor"
    )
    attn_cols = lax.psum_scatter(
        head_terms(context, output_weight).astype(jnp.bfloat16),
        "tensor",
        scatter_dimension=1,
        tiled=True,
    ).astype(jnp.float32)
    col_count = attn_cols.shape[1]
    up_weight_columns = lax.dynamic_slice_in_dim(
        up_weight_single, tensor_rank * col_count, col_count, 1
    )
    hidden_states = (
        residual.astype(jnp.float32)
        + attn_cols
        + ADAPTER_SCALE * jnp.dot(reduced_state, up_weight_columns, precision=lax.Precision.HIGHEST)
    )
    target = residual.astype(jnp.float32) + frozen_residual_delta.astype(jnp.float32)
    gap = hidden_states - target
    sq_state, sq_target, cross_term, gap_sq = lax.psum(
        (
            jnp.sum(hidden_states * hidden_states, axis=1),
            jnp.sum(target * target, axis=1),
            jnp.sum(hidden_states * target, axis=1),
            jnp.sum(gap * gap, axis=1),
        ),
        "tensor",
    )
    positions = jnp.arange(seq_len, dtype=jnp.int32)
    harmful, retained = token_masks(positions, harm_here, keep_here)
    output_gradient = row_gradient(
        hidden_states,
        target,
        sq_state,
        sq_target,
        cross_term,
        gap_sq,
        harmful,
        retained,
        harm_total,
        keep_total,
    )
    reduced_gradient = lax.psum(
        ADAPTER_SCALE
        * jnp.dot(output_gradient, up_weight_columns.T, precision=lax.Precision.HIGHEST),
        "tensor",
    )
    local_a = jnp.dot(
        context.T,
        reduced_gradient,
        precision=lax.Precision.HIGHEST,
        preferred_element_type=jnp.float32,
    )
    shard_up_weight = ADAPTER_SCALE * jnp.dot(
        reduced_state.T, output_gradient, precision=lax.Precision.HIGHEST
    )
    grad_a, grad_b_cols = lax.psum((local_a, shard_up_weight), "dp")
    grad_b = lax.all_gather(grad_b_cols, "tensor", axis=1, tiled=True)
    adapted = hidden_states.astype(jnp.bfloat16)
    return (adapted, grad_a, grad_b)


def solution(mesh):
    return jax.shard_map(
        local,
        mesh=mesh,
        in_specs=(
            P("dp", "tensor"),
            P("tensor", "dp"),
            P("tensor", None),
            P(),
            P("dp", "tensor"),
            P("dp", "tensor"),
            P(),
            P(),
        ),
        out_specs=(P("dp", "tensor"), P("tensor", None), P()),
        check_vma=False,
    )
```

profile of v0, /device:TPU:2, one launch (start us, length us, event | category | flops | bytes accessed | tf_op | source)
XLA Modules:
  0.0 659.6 jit_solution(2326122769122141415)
XLA Ops:
  7.2 0.0 copy-start
  7.2 0.0 all-gather.2.cloned.1.call-start
  7.2 0.7 all-gather.2.cloned.1.call-update
  7.9 0.0 reduce-scatter.2.cloned.1.call-start
  8.0 156.6 %all-gather.2.cloned.1.call-done = bf16[1024,8192]{1,0:T(8,128)(2,1)} async-done(((bf16[1024,256]{1,0:T(8,128)(2,1)}), bf16[1024,8192]{1,0:T(8,128)(2,1)}) %all-gather.2.cloned.1.call-update) | async-done | bytes 16777232 | tf_op jit(solution)/shard_map/all_gather | solution.py:45
  164.5 0.0 copy-done
  164.5 14.3 %convolution_convert_fusion = bf16[384,8192]{1,0:T(8,128)(2,1)} fusion(bf16[384,1024]{1,0:T(8,128)(2,1)S(1)} %copy-done, bf16[1024,8192]{1,0:T(8,128)(2,1)} %all-gather.2.cloned.1.call-done), kind=kOutput, calls=%fused_computation | convolution fusion | flops 6445596672 | bytes 23855104 | tf_op jit(solution)/shard_map/dot_general | solution.py:43
  178.9 0.0 copy-start.3
  178.9 0.0 copy-start.4
  178.9 0.0 copy-start.2
  178.9 0.0 copy-start.1
  178.9 0.0 reduce-scatter.2.cloned.1.call-update
  178.9 0.0 all-reduce.4.cloned.1.call-start
  179.0 0.6 copy-done.3
  179.5 0.6 reduce_sum.58
  180.2 0.6 dynamic_slice.11
  180.8 0.0 copy-done.4
  180.8 0.6 reduce_sum.54
  181.5 0.6 dynamic_slice.10
  184.7 0.0 copy-done.2
  184.7 0.3 fusion.8
  185.0 32.4 %psum.56 = f32[384,16]{0,1:T(8,128)S(1)} all-reduce(f32[384,16]{0,1:T(8,128)S(1)} %fusion.8), channel_id=1, replica_groups=mesh['dp'=32,'tensor'=8] {'tensor'}, use_global_device_ids=true, to_apply=%region_1.0 | all-reduce | flops 6144 | bytes 49152 | tf_op jit(solution)/shard_map/psum | solution.py:68
  217.4 92.1 %reduce-scatter.2.cloned.1.call-done = bf16[384,1024]{1,0:T(8,128)(2,1)} async-done(((bf16[384,8192]{1,0:T(8,128)(2,1)}), bf16[384,1024]{1,0:T(8,128)(2,1)}) %reduce-scatter.2.cloned.1.call-update) | async-done | bytes 786448 | tf_op jit(solution)/shard_map/reduce_scatter | solution.py:71
  309.5 0.0 copy-done.1
  309.5 3.1 multiply_reduce_fusion.1
  312.6 17.1 %all-reduce.1 = (f32[384]{0:T(512)S(1)}, f32[384]{0:T(512)S(1)}, f32[384]{0:T(512)S(1)}, f32[384]{0:T(512)S(1)}) all-reduce(f32[384]{0:T(512)S(1)} %get-tuple-element.4, f32[384]{0:T(512)S(1)} %get-tuple-element.3, f32[384]{0:T(512)S(1)} %get-tuple-element.6, f32[384]{0:T(512)S(1)} %get-tuple-element.5), channel_id=1, replica_groups=mesh['dp'=32,'tensor'=8] {'tensor'}, use_global_device_ids=true, to_apply=%region_11.0 | all-reduce | flops 1536 | bytes 12288 | tf_op jit(solution)/shard_map/psum | solution.py:88
  329.8 0.7 select_divide_fusion
  330.4 2.7 multiply_add_fusion
  333.1 1.5 convolution_multiply_fusion.1
  334.6 1.6 convolution_multiply_fusion
  336.2 33.9 %psum.61 = f32[384,16]{1,0:T(8,128)S(1)} all-reduce(f32[384,16]{1,0:T(8,128)S(1)} %convolution_multiply_fusion), channel_id=1, replica_groups=mesh['dp'=32,'tensor'=8] {'tensor'}, use_global_device_ids=true, to_apply=%region_12.0 | all-reduce | flops 6144 | bytes 49152 | tf_op jit(solution)/shard_map/psum | solution.py:111
  370.2 1.1 convolution_bitcast_fusion
  371.3 0.0 all-reduce.4.cloned.1.call-update
  371.3 249.6 %all-reduce.4.cloned.1.call-done = (f32[1024,16]{0,1:T(8,128)}, f32[16,1024]{1,0:T(8,128)}) async-done(((f32[1024,16]{0,1:T(8,128)}, f32[16,1024]{1,0:T(8,128)}), (f32[1024,16]{0,1:T(8,128)}, f32[16,1024]{1,0:T(8,128)})) %all-reduce.4.cloned.1.call-update) | async-done | bytes 131088 | tf_op jit(solution)/shard_map/psum | solution.py:125
  620.9 29.9 %all_gather.7 = f32[16,8192]{1,0:T(8,128)S(1)} all-gather(f32[16,1024]{1,0:T(8,128)} %get-tuple-element.8), channel_id=1, replica_groups=mesh['dp'=32,'tensor'=8] {'tensor'}, dimensions={1}, use_global_device_ids=true | all-gather | bytes 589824 | tf_op jit(solution)/shard_map/all_gather | solution.py:126
  650.8 1.5 copy.14
  652.3 0.8 copy.15
Async XLA Ops:
  7.2 157.4 %copy-start = (bf16[384,1024]{1,0:T(8,128)(2,1)S(1)}, bf16[384,1024]{1,0:T(8,128)(2,1)}, u32[]{:S(2)}) copy-start(bf16[384,1024]{1,0:T(8,128)(2,1)} %param.8) | copy-start | bytes 2359300
  7.2 157.4 %all-gather.2.cloned.1.call-start = ((), (), s32[]{:S(2)}) async-start(), calls=%async_computation.1 | async-start | bytes 17301504 | tf_op jit(solution)/shard_map/all_gather | solution.py:45
  7.9 301.6 %reduce-scatter.2.cloned.1.call-start = ((), (), s32[]{:S(2)}) async-start(), calls=%async_computation.2 | async-start | bytes 7077888 | tf_op jit(solution)/shard_map/reduce_scatter | solution.py:71
  178.9 0.7 copy-start.3
  178.9 1.9 copy-start.4
  178.9 5.8 copy-start.2
  178.9 130.6 %copy-start.1 = (bf16[384,1024]{1,0:T(8,128)(2,1)S(1)}, bf16[384,1024]{1,0:T(8,128)(2,1)}, u32[]{:S(2)}) copy-start(bf16[384,1024]{1,0:T(8,128)(2,1)} %param.13) | copy-start | bytes 2359300
  178.9 442.0 %all-reduce.4.cloned.1.call-start = ((), (), s32[]{:S(2)}) async-start(), calls=%async_computation.3 | async-start | bytes 262144 | tf_op jit(solution)/shard_map/psum | solution.py:125
Sparse Core Ops, SparseCore 0:
  10.5 153.9 all-gather.1
  179.0 130.3 reduce-scatter.1
  371.4 249.4 all-reduce.3
where the time goes:
time: 660 us
  waiting for transfers between devices  499 us (76%)
  blocking collectives  113 us (17%)
  matrix products  22 us (3%)
  between operations  16.5 us (2%)
    psum x1, waiting for transfers between devices, local(): grad_a, grad_b_cols = lax.psum((local_a, shard_up_weight), 'dp')  250 us
    all_gather x1, waiting for transfers between devices, head_terms(): lax.all_gather(output_weight, 'dp', axis=1, tiled=True)  157 us
    reduce_scatter x1, waiting for transfers between devices, local(): lax.psum_scatter(head_terms(context, output_weight).astype(jnp.bfloat16),...  92.1 us
    psum x1, blocking collectives, local(): lax.psum(ADAPTER_SCALE * jnp.dot(output_gradient, up_weight_columns.T, pr...  33.9 us
    psum x1, blocking collectives, local(): lax.psum(jnp.dot(context, adapter_down_weight, preferred_element_type=jnp...  32.4 us
    all_gather x1, blocking collectives, local(): grad_b = lax.all_gather(grad_b_cols, 'tensor', axis=1, tiled=True)  29.9 us
    psum x1, blocking collectives, local(): lax.psum((jnp.sum(hidden_states * hidden_states, axis=1), jnp.sum(target...  17.1 us
    dot_general x1, matrix products, head_terms(): jnp.dot(context, lax.all_gather(output_weight, 'dp', axis=1, tiled=True),...  14.3 us
  transfers between devices with their start and end apart: 3, of which 3 were waited for; matrix products, arithmetic and copies ran while one was open for 0% of the time, Pallas kernels for 0%

commit v1 on v0

--- a/solution.py
+++ b/solution.py
@@ -42,7 +42,9 @@
 def head_terms(context, output_weight):
     return jnp.dot(
         context,
-        lax.all_gather(output_weight, "dp", axis=1, tiled=True),
+        jnp.concatenate(
+            lax.all_to_all(jnp.stack([output_weight] * lax.axis_size("dp")), "dp", 0, 0), axis=1
+        ),
         preferred_element_type=jnp.float32,
     )
 

time: 660 us -> 881 us (1.33)
  blocking collectives: 113 us -> 490 us
  waiting for transfers between devices: 499 us -> 342 us
    all_to_all x0 -> x1, blocking collectives: none -> 376 us  [head_terms(): lax.all_to_all(jnp.stack([output_weight] * lax.axis_size('dp')), 'dp', 0, 0)]
    all_gather x1 -> x0, waiting for transfers between devices: 157 us -> none  [head_terms(): lax.all_gather(output_weight, 'dp', axis=1, tiled=True)]
  transfers between devices with their start and end apart: 3 -> 2, of which waited for: 3 -> 2; matrix products, arithmetic and copies ran while one was open for 0% -> 0% of each run, Pallas kernels for 0% -> 0%
where the time goes in v1:
time: 881 us
  blocking collectives  490 us (56%)
  waiting for transfers between devices  342 us (39%)
  matrix products  19.6 us (2%)
  between operations  16.8 us (2%)
    all_to_all x1, blocking collectives, head_terms(): lax.all_to_all(jnp.stack([output_weight] * lax.axis_size('dp')), 'dp', 0, 0)  376 us
    psum x1, waiting for transfers between devices, local(): grad_a, grad_b_cols = lax.psum((local_a, shard_up_weight), 'dp')  250 us
    reduce_scatter x1, waiting for transfers between devices, local(): lax.psum_scatter(head_terms(context, output_weight).astype(jnp.bfloat16),...  92.7 us
    psum x1, blocking collectives, local(): lax.psum(ADAPTER_SCALE * jnp.dot(output_gradient, up_weight_columns.T, pr...  33.9 us
    psum x1, blocking collectives, local(): lax.psum(jnp.dot(context, adapter_down_weight, preferred_element_type=jnp...  32.7 us
    all_gather x1, blocking collectives, local(): grad_b = lax.all_gather(grad_b_cols, 'tensor', axis=1, tiled=True)  29.9 us
  transfers between devices with their start and end apart: 2, of which 2 were waited for; matrix products, arithmetic and copies ran while one was open for 0% of the time, Pallas kernels for 0%

profile of v1, /device:TPU:2, one launch (start us, length us, event | category | flops | bytes accessed | tf_op | source)
XLA Modules:
  0.0 880.8 jit_solution(729789084789001168)
XLA Ops:
  7.2 0.0 copy-start
  7.2 0.0 reduce-scatter.2.cloned.1.call-start
  7.2 1.3 copy.11
  8.5 2.2 stack.2
  10.7 376.0 %all_to_all.5 = bf16[32,1024,256]{1,2,0:T(8,128)(2,1)} all-to-all(bf16[32,1024,256]{1,2,0:T(8,128)(2,1)S(1)} %stack.2), channel_id=1, replica_groups=mesh['dp'=32,'tensor'=8] {'dp'}, dimensions={0} | all-to-all | bytes 33554432 | tf_op jit(solution)/shard_map/all_to_all | solution.py:46
  386.7 0.0 copy-done
  386.7 12.0 %convolution_convert_fusion = bf16[384,8192]{1,0:T(8,128)(2,1)} fusion(bf16[384,1024]{1,0:T(8,128)(2,1)S(1)} %copy-done, bf16[1024,8192]{0,1:T(8,128)(2,1)} %bitcast.17), kind=kOutput, calls=%fused_computation | convolution fusion | flops 6445596672 | bytes 23855104 | tf_op jit(solution)/shard_map/dot_general | solution.py:43
  398.7 0.0 copy-start.3
  398.7 0.0 copy-start.4
  398.7 0.0 copy-start.2
  398.7 0.0 copy-start.1
  398.7 0.0 reduce-scatter.2.cloned.1.call-update
  398.7 0.0 all-reduce.4.cloned.1.call-start
  398.8 0.6 copy-done.3
  399.3 0.6 reduce_sum.54
  399.9 0.6 dynamic_slice.10
  400.5 0.0 copy-done.4
  400.5 0.6 dynamic_slice.11
  401.2 0.6 reduce_sum.58
  404.5 0.0 copy-done.2
  404.5 0.3 fusion.8
  404.8 32.7 %psum.56 = f32[384,16]{0,1:T(8,128)S(1)} all-reduce(f32[384,16]{0,1:T(8,128)S(1)} %fusion.8), channel_id=1, replica_groups=mesh['dp'=32,'tensor'=8] {'tensor'}, use_global_device_ids=true, to_apply=%region_1.0 | all-reduce | flops 6144 | bytes 49152 | tf_op jit(solution)/shard_map/psum | solution.py:70
  437.5 92.7 %reduce-scatter.2.cloned.1.call-done = bf16[384,1024]{1,0:T(8,128)(2,1)} async-done(((bf16[384,8192]{1,0:T(8,128)(2,1)}), bf16[384,1024]{1,0:T(8,128)(2,1)}) %reduce-scatter.2.cloned.1.call-update) | async-done | bytes 786448 | tf_op jit(solution)/shard_map/reduce_scatter | solution.py:73
  530.1 0.0 copy-done.1
  530.1 3.1 multiply_reduce_fusion.1
  533.3 17.2 %all-reduce.1 = (f32[384]{0:T(512)S(1)}, f32[384]{0:T(512)S(1)}, f32[384]{0:T(512)S(1)}, f32[384]{0:T(512)S(1)}) all-reduce(f32[384]{0:T(512)S(1)} %get-tuple-element.4, f32[384]{0:T(512)S(1)} %get-tuple-element.3, f32[384]{0:T(512)S(1)} %get-tuple-element.6, f32[384]{0:T(512)S(1)} %get-tuple-element.5), channel_id=1, replica_groups=mesh['dp'=32,'tensor'=8] {'tensor'}, use_global_device_ids=true, to_apply=%region_11.0 | all-reduce | flops 1536 | bytes 12288 | tf_op jit(solution)/shard_map/psum | solution.py:90
  550.5 0.7 select_divide_fusion
  551.2 2.7 multiply_add_fusion
  553.9 1.6 convolution_multiply_fusion
  555.5 1.5 convolution_multiply_fusion.1
  557.0 33.9 %psum.61 = f32[384,16]{1,0:T(8,128)S(1)} all-reduce(f32[384,16]{1,0:T(8,128)S(1)} %convolution_multiply_fusion), channel_id=1, replica_groups=mesh['dp'=32,'tensor'=8] {'tensor'}, use_global_device_ids=true, to_apply=%region_12.0 | all-reduce | flops 6144 | bytes 49152 | tf_op jit(solution)/shard_map/psum | solution.py:113
  590.9 1.1 convolution_bitcast_fusion
  592.0 0.0 all-reduce.4.cloned.1.call-update
  592.0 249.8 %all-reduce.4.cloned.1.call-done = (f32[1024,16]{0,1:T(8,128)}, f32[16,1024]{1,0:T(8,128)}) async-done(((f32[1024,16]{0,1:T(8,128)}, f32[16,1024]{1,0:T(8,128)}), (f32[1024,16]{0,1:T(8,128)}, f32[16,1024]{1,0:T(8,128)})) %all-reduce.4.cloned.1.call-update) | async-done | bytes 131088 | tf_op jit(solution)/shard_map/psum | solution.py:127
  841.8 29.9 %all_gather.3 = f32[16,8192]{1,0:T(8,128)S(1)} all-gather(f32[16,1024]{1,0:T(8,128)} %get-tuple-element.8), channel_id=1, replica_groups=mesh['dp'=32,'tensor'=8] {'tensor'}, dimensions={1}, use_global_device_ids=true | all-gather | bytes 589824 | tf_op jit(solution)/shard_map/all_gather | solution.py:128
  871.7 1.5 copy.15
  873.2 0.8 copy.16
Async XLA Ops:
  7.2 379.5 %copy-start = (bf16[384,1024]{1,0:T(8,128)(2,1)S(1)}, bf16[384,1024]{1,0:T(8,128)(2,1)}, u32[]{:S(2)}) copy-start(bf16[384,1024]{1,0:T(8,128)(2,1)} %param.8) | copy-start | bytes 2359300
  7.2 522.9 %reduce-scatter.2.cloned.1.call-start = ((), (), s32[]{:S(2)}) async-start(), calls=%async_computation.2 | async-start | bytes 7077888 | tf_op jit(solution)/shard_map/reduce_scatter | solution.py:73
  398.7 0.7 copy-start.3
  398.7 1.9 copy-start.4
  398.7 5.8 copy-start.2
  398.7 131.5 %copy-start.1 = (bf16[384,1024]{1,0:T(8,128)(2,1)S(1)}, bf16[384,1024]{1,0:T(8,128)(2,1)}, u32[]{:S(2)}) copy-start(bf16[384,1024]{1,0:T(8,128)(2,1)} %param.13) | copy-start | bytes 2359300
  398.7 443.1 %all-reduce.4.cloned.1.call-start = ((), (), s32[]{:S(2)}) async-start(), calls=%async_computation.3 | async-start | bytes 262144 | tf_op jit(solution)/shard_map/psum | solution.py:127
Sparse Core Ops, SparseCore 0:
  398.8 131.2 reduce-scatter.1
  592.1 249.6 all-reduce.3
